TPU v7x, 32 devices: a whole 2x2x4 slice. The times are simulated.
32 devices in a mesh: survey: 2 (over x), sector: 16 (over z, y, core).
Axes of the slice: x: 2, y: 2, z: 4, core: 2. Of those that a mesh axis runs over, the one named last changes fastest.
Arguments:
- raw_pings: bfloat16 [32, 512, 2, 1024], P('survey', 'sector'), parts along dimension 0, may hold values from -6 to 6
- focus_matrix: bfloat16 [2, 2048, 512], replicated, may hold values from -0.25 to 0.25
- start_angle: int32 [32], P('survey'), parts along dimension 0, may hold values from 0 to 2047
- ping_count: int32 [32], P('survey'), parts along dimension 0, may hold values from 256 to 512, as said below
Outputs:
- coherence: float32 [32, 2048, 1024], P(('survey', 'sector')), parts along dimension 0
- interferogram: bfloat16 [32, 2, 2048, 1024], P(('survey', 'sector')), parts along dimension 0
There are 2 independent parts, one for each index of `survey`. A program takes and returns all parts, laid end to end along the dimension named above; an argument that names none is the same for every part. Nothing has to cross between parts.
Inputs may be any that keep to these rules, and one draw needn't show every extreme that they name: `ping_count`: every value lies between 256 and 512, and at least one sector holds all 512 pings.
All inputs are finite; a program needn't handle non-finite values.
Results may differ from a plain program's by a relative error of at most 0.0057.
Values may be sent and summed in bfloat16 or wider, within the bound.
No kernel may reach another device: no remote copies, remote signals or barrier semaphores. Data moves between devices by JAX's collectives and lax.ppermute only.
A program may use at most 192 MiB of HBM per device.

v0:
```python
import jax
import jax.numpy as jnp
from jax import lax
from jax.sharding import PartitionSpec as P

WIN = 9


def shifted(block, axis, distance):
    devices = range(lax.axis_size(axis))
    route = [((i - distance) % len(devices), i) for i in devices]
    return lax.ppermute(block, axis, route)


def focus_sector(raw, angle_step, valid_pings, stacked):
    pings_here = raw.shape[0]
    ranges_here = raw.shape[2]
    columns_count = stacked.shape[0] // 2
    ping_mask = (jnp.arange(pings_here, dtype=jnp.int32) < valid_pings).astype(jnp.bfloat16)
    masked = raw * ping_mask[:, None, None]
    product = jnp.dot(
        stacked, masked.reshape(pings_here, 2 * ranges_here), preferred_element_type=jnp.float32
    )
    product = product.reshape(2, columns_count, 2, ranges_here)
    real_part = product[0, :, 0] - product[1, :, 1]
    imag_part = product[0, :, 1] + product[1, :, 0]
    columns = jnp.arange(columns_count, dtype=jnp.int32)
    turn_index = angle_step * columns % columns_count
    phase_turn = 2.0 * jnp.pi / columns_count * turn_index.astype(jnp.float32)
    cosine = jnp.cos(phase_turn)[:, None]
    sine_part = jnp.sin(phase_turn)[:, None]
    mean_power = jnp.mean(real_part * real_part + imag_part * imag_part, axis=0)
    inverse_rms = lax.rsqrt(mean_power + 1e-06)
    turned_real = (real_part * cosine + imag_part * sine_part) * inverse_rms
    turned_imag = (imag_part * cosine - real_part * sine_part) * inverse_rms
    return jnp.stack([turned_real, turned_imag], axis=1).astype(jnp.bfloat16)


def window_sum(field, axis, span):
    half_span = span // 2
    length_axis = field.shape[axis]
    widths = [(0, 0)] * field.ndim
    widths[axis] = (half_span, half_span)
    padded = jnp.pad(field, widths)
    total = lax.slice_in_dim(padded, 0, length_axis, axis=axis)
    for offset in range(1, span):
        total = total + lax.slice_in_dim(padded, offset, offset + length_axis, axis=axis)
    return total


def compare(own_image, other_image, span):
    f_real = own_image[:, 0].astype(jnp.float32)
    f_imag = own_image[:, 1].astype(jnp.float32)
    g_real = other_image[:, 0].astype(jnp.float32)
    g_imag = other_image[:, 1].astype(jnp.float32)
    fields = jnp.stack(
        [
            f_real * g_real + f_imag * g_imag,
            f_imag * g_real - f_real * g_imag,
            f_real * f_real + f_imag * f_imag,
            g_real * g_real + g_imag * g_imag,
        ],
        axis=0,
    )
    looked = window_sum(window_sum(fields, 1, span), 2, span)
    magnitude = jnp.sqrt(looked[0] * looked[0] + looked[1] * looked[1])
    energy = jnp.sqrt(looked[2] * looked[3] + 1e-06)
    coherence = magnitude / energy
    interferogram = (looked[0:2] / float(span * span)).astype(jnp.bfloat16)
    return (coherence, interferogram)


def body(raw_pings, focus_matrix, start_angle, ping_count):
    stacked = focus_matrix.reshape(2 * focus_matrix.shape[1], focus_matrix.shape[2])
    position = lax.axis_index("sector")

    def prepare(pieces, sector):
        return focus_sector(pieces[0], start_angle[sector], ping_count[sector], stacked)[None]

    own_image = (lambda pieces: prepare(pieces, position))(
        lax.all_to_all(raw_pings, "sector", split_axis=0, concat_axis=1, tiled=True)
    )
    other_image = shifted(own_image, "sector", -1)
    coherence, interferogram = compare(own_image[0], other_image[0], WIN)
    return (coherence[None], interferogram[None])


def solution(mesh):
    return jax.shard_map(
        body,
        mesh=mesh,
        in_specs=(P("survey", "sector", None, None), P(), P("survey"), P("survey")),
        out_specs=(P(("survey", "sector"), None, None), P(("survey", "sector"), None, None, None)),
        check_vma=False,
    )
```

profile of v0, /device:TPU:0, one launch (start us, length us, event | category | flops | bytes accessed | tf_op | source)
XLA Modules:
  0.0 722.9 jit_solution(4973740520128592052)
XLA Ops:
  0.6 7.4 %all-to-all-start = ((bf16[16,32,2,1024]{3,2,1,0:T(2,128)(2,1)}), bf16[16,32,2,1024]{3,2,1,0:T(2,128)(2,1)S(1)}, u32[]{:S(2)}, u32[]{:S(2)}) async-start(bf16[16,32,2,1024]{3,2,1,0:T(2,128)(2,1)} %param.4), calls=%async_computation | async-start | bytes 4194304 | tf_op jit(solution)/shard_map/all_to_all | solution.py:81
  8.1 1.2 dynamic_slice.6
  9.3 1.2 dynamic_slice.7
  10.5 0.7 fusion.37
  11.2 0.7 fusion.38
  11.9 37.1 %all-to-all-done = bf16[16,32,2,1024]{3,2,1,0:T(2,128)(2,1)S(1)} async-done(((bf16[16,32,2,1024]{3,2,1,0:T(2,128)(2,1)}), bf16[16,32,2,1024]{3,2,1,0:T(2,128)(2,1)S(1)}, u32[]{:S(2)}, u32[]{:S(2)}) %all-to-all-start) | async-done | bytes 2097184 | tf_op jit(solution)/shard_map/all_to_all | solution.py:81
  49.0 1.9 broadcast_multiply_fusion
  50.9 0.6 copy.14
  51.5 17.5 %convolution_bitcast_fusion = f32[4096,2048]{0,1:T(8,128)} fusion(bf16[512,2048]{1,0:T(8,128)(2,1)S(1)} %bitcast.52, bf16[4096,512]{1,0:T(8,128)(2,1)} %bitcast.53), kind=kOutput, calls=%fused_computation.23 | convolution fusion | flops 8589934592 | bytes 39845888 | tf_op jit(solution)/shard_map/dot_general | solution.py:21
  69.0 42.6 %reshape.411 = f32[2,2048,2,1024]{1,0,3,2:T(2,128)} reshape(f32[4096,2048]{0,1:T(8,128)} %convolution_bitcast_fusion) | data formatting | bytes 67108864 | tf_op jit(solution)/shard_map/reshape | solution.py:24
  111.7 39.8 %fusion.42 = (f32[1,2048,1,1024]{1,0,3,2:T(1,128)}, f32[1,2048,1,1024]{1,0,3,2:T(1,128)}, f32[1,2048,1,1024]{1,0,3,2:T(1,128)}, f32[1,2048,1,1024]{1,0,3,2:T(1,128)}) fusion(f32[2,2048,2,1024]{1,0,3,2:T(2,128)} %reshape.411), kind=kLoop, calls=%fused_computation.80 | loop fusion | bytes 67108864 | tf_op jit(solution)/shard_map/slice | solution.py:25
  151.5 20.7 %copy.10 = f32[1,2048,1,1024]{3,1,2,0:T(8,128)} copy(f32[1,2048,1,1024]{1,0,3,2:T(1,128)} %get-tuple-element.10) | data formatting | bytes 16777216
  172.3 20.7 %copy.11 = f32[1,2048,1,1024]{3,1,2,0:T(8,128)} copy(f32[1,2048,1,1024]{1,0,3,2:T(1,128)} %get-tuple-element.8) | data formatting | bytes 16777216
  192.9 20.5 %copy.12 = f32[1,2048,1,1024]{3,1,2,0:T(8,128)} copy(f32[1,2048,1,1024]{1,0,3,2:T(1,128)} %get-tuple-element.9) | data formatting | bytes 16777216
  213.5 20.5 %copy.13 = f32[1,2048,1,1024]{3,1,2,0:T(8,128)} copy(f32[1,2048,1,1024]{1,0,3,2:T(1,128)} %get-tuple-element.11) | data formatting | bytes 16777216
  234.0 19.2 %add_reduce_fusion = (f32[1024]{0:T(1024)S(1)}, f32[1,2048,1,1024]{3,1,2,0:T(8,128)}, f32[1,2048,1,1024]{3,1,2,0:T(8,128)}) fusion(f32[1,2048,1,1024]{3,1,2,0:T(8,128)} %copy.12, f32[1,2048,1,1024]{3,1,2,0:T(8,128)} %copy.13, f32[1,2048,1,1024]{3,1,2,0:T(8,128)} %copy.10, f32[1,2048,1,1024]{3,1,2,0:T(8,128)} %copy.11), kind=kLoop, calls=%fused_computation.64 | loop fusion | flops 12581888 | bytes 50335744 | tf_op jit(solution)/shard_map/reduce_sum | solution.py:32
  253.3 8.6 %multiply_convert_fusion.1 = (bf16[1,2048,1,1024]{3,1,2,0:T(8,128)(2,1)S(1)}, bf16[1,2048,1,1024]{3,1,2,0:T(8,128)(2,1)}) fusion(f32[1,2048,1,1024]{3,1,2,0:T(8,128)} %get-tuple-element.6, f32[1,2048,1,1024]{3,1,2,0:T(8,128)} %get-tuple-element.7, f32[1024]{0:T(1024)S(1)} %add_rsqrt_fusion, f32[2048]{0:T(1024)S(1)} %get-tuple-element.17, ...), kind=kLoop, calls=%fused_computation.63 | loop fusion | flops 20971520 | bytes 25186304 | tf_op jit(solution)/shard_map/convert
  261.9 6.2 pad_maximum_fusion.1
  268.0 9.8 %collective-permute-start = (bf16[1,2048,2,1024]{3,1,2,0:T(8,128)(2,1)}, bf16[1,2048,2,1024]{3,1,2,0:T(8,128)(2,1)S(1)}, u32[]{:S(2)}, u32[]{:S(2)}) collective-permute-start(bf16[1,2048,2,1024]{3,1,2,0:T(8,128)(2,1)} %pad_maximum_fusion.1), channel_id=1, source_target_pairs={{1,0},{2,1},{3,2},{4,3},{5,4},{6,5},{7,6},{8,7},{9,8},{10,9},{11,1... | collective-permute-start | bytes 25165832 | tf_op jit(solution)/shard_map/ppermute | solution.py:12
  277.9 91.3 %collective-permute-done = bf16[1,2048,2,1024]{3,1,2,0:T(8,128)(2,1)S(1)} collective-permute-done((bf16[1,2048,2,1024]{3,1,2,0:T(8,128)(2,1)}, bf16[1,2048,2,1024]{3,1,2,0:T(8,128)(2,1)S(1)}, u32[]{:S(2)}, u32[]{:S(2)}) %collective-permute-start) | collective-permute-done | bytes 8388640 | tf_op jit(solution)/shard_map/ppermute | solution.py:12
  369.2 13.3 %fusion.14 = (f32[1,2048,1024]{2,1,0:T(8,128)}, bf16[2048,1,1024]{2,0,1:T(8,128)(2,1)S(1)}, bf16[2048,1,1024]{2,0,1:T(8,128)(2,1)}) fusion(bf16[2048,2,1024]{2,0,1:T(8,128)(2,1)S(1)} %bitcast.49, f32[1024]{0:T(1024)S(1)} %add_rsqrt_fusion, f32[2048]{0:T(1024)S(1)} %get-tuple-element.17, f32[1,2048,1,1024]{3,1,2,0:T(8,128)} %get-tuple-element.7, ...), kind=kLoop, calls=%fused_computation.37 | loop fusion | flops 35651584 | bytes 41963520 | tf_op jit(solution)/shard_map/add | solution.py:58
  382.5 11.1 %fusion.18 = (f32[1,2048,1024]{2,1,0:T(8,128)}, f32[1,2048,1024]{2,1,0:T(8,128)}, f32[1,2048,1024]{2,1,0:T(8,128)}) fusion(bf16[2048,1,1024]{2,0,1:T(8,128)(2,1)S(1)} %get-tuple-element.3, bf16[2048,1,1024]{2,0,1:T(8,128)(2,1)} %get-tuple-element.4, bf16[2048,2,1024]{2,0,1:T(8,128)(2,1)S(1)} %bitcast.50), kind=kLoop, calls=%fused_computation.41 | loop fusion | flops 27262976 | bytes 41943040 | tf_op jit(solution)/shard_map/sub | solution.py:59
  393.6 23.4 %pad_maximum_fusion = f32[4,2048,1024]{2,1,0:T(8,128)} fusion(f32[1,2048,1024]{2,1,0:T(8,128)} %get-tuple-element.15, f32[1,2048,1024]{2,1,0:T(8,128)} %get-tuple-element.16, f32[1,2048,1024]{2,1,0:T(8,128)} %get-tuple-element.14, f32[1,2048,1024]{2,1,0:T(8,128)} %get-tuple-element.2), kind=kLoop, calls=%fused_computation.16 | loop fusion | flops 25165824 | bytes 67108864 | tf_op jit(solution)/shard_map/stack | solution.py:56
  417.0 131.8 %slice_add_fusion = f32[4,2048,1024]{2,1,0:T(8,128)} fusion(f32[4,2048,1024]{2,1,0:T(8,128)} %pad_maximum_fusion), kind=kLoop, calls=%fused_computation.17 | loop fusion | flops 67108864 | bytes 67108864 | tf_op jit(solution)/shard_map/add | solution.py:47
  548.8 147.7 %fusion.7 = f32[4,2048,1024]{2,1,0:T(8,128)} fusion(f32[4,2048,1024]{2,1,0:T(8,128)} %slice_add_fusion), kind=kLoop, calls=%fused_computation.15 | loop fusion | flops 67108864 | bytes 67108864 | tf_op jit(solution)/shard_map/add | solution.py:47
  696.5 9.6 %fusion.19 = bf16[1,2,2048,1024]{3,2,1,0:T(8,128)(2,1)} fusion(f32[4,2048,1024]{2,1,0:T(8,128)} %fusion.7), kind=kLoop, calls=%fused_computation.42 | loop fusion | flops 8388608 | bytes 25165824 | tf_op jit(solution)/shard_map/broadcast_in_dim | solution.py:85
  706.1 16.7 %fusion.22 = f32[1,2048,1024]{2,1,0:T(8,128)} fusion(f32[4,2048,1024]{2,1,0:T(8,128)} %fusion.7), kind=kLoop, calls=%fused_computation.46 | loop fusion | flops 12582912 | bytes 41943040 | tf_op jit(solution)/shard_map/div | solution.py:68
  (1 shorter events, 0.0 us)
Async XLA Ops:
  0.6 48.4 %all-to-all-start = ((bf16[16,32,2,1024]{3,2,1,0:T(2,128)(2,1)}), bf16[16,32,2,1024]{3,2,1,0:T(2,128)(2,1)S(1)}, u32[]{:S(2)}, u32[]{:S(2)}) async-start(bf16[16,32,2,1024]{3,2,1,0:T(2,128)(2,1)} %param.4), calls=%async_computation | async-start | bytes 4194304 | tf_op jit(solution)/shard_map/all_to_all | solution.py:81
  268.0 101.1 %collective-permute-start = (bf16[1,2048,2,1024]{3,1,2,0:T(8,128)(2,1)}, bf16[1,2048,2,1024]{3,1,2,0:T(8,128)(2,1)S(1)}, u32[]{:S(2)}, u32[]{:S(2)}) collective-permute-start(bf16[1,2048,2,1024]{3,1,2,0:T(8,128)(2,1)} %pad_maximum_fusion.1), channel_id=1, source_target_pairs={{1,0},{2,1},{3,2},{4,3},{5,4},{6,5},{7,6},{8,7},{9,8},{10,9},{11,1... | collective-permute-start | bytes 25165832 | tf_op jit(solution)/shard_map/ppermute | solution.py:12
where the time goes:
time: 726 us; the launch traced here: 723 us
  other arithmetic  391 us (54%)
  local copies, waits for them, and re-layouts  168 us (23%)
  waiting for transfers between devices  128 us (18%)
  matrix products  17.5 us (2%)
  starting transfers between devices  17.3 us (2%)
    add x2, other arithmetic, window_sum(): total + lax.slice_in_dim(padded, offset, offset + length_axis, axis=axis)  280 us
    ppermute x1, waiting for transfers between devices, shifted(): return lax.ppermute(block, axis, route)  91.3 us
    unnamed x5, local copies, waits for them, and re-layouts  83.1 us
    reshape x1, local copies, waits for them, and re-layouts, focus_sector(): product = product.reshape(2, columns_count, 2, ranges_here)  42.6 us
    slice x1, local copies, waits for them, and re-layouts, focus_sector(): real_part = product[0, :, 0] - product[1, :, 1]  39.8 us
    all_to_all x1, waiting for transfers between devices, body(): lax.all_to_all(raw_pings, 'sector', split_axis=0, concat_axis=1, tiled=True)  37.1 us
    another operation x1, other arithmetic, compare(): jnp.stack([f_real * g_real + f_imag * g_imag, f_imag * g_real - f_real *...  23.4 us
    reduce_sum x1, other arithmetic, focus_sector(): mean_power = jnp.mean(real_part * real_part + imag_part * imag_part, axis=0)  19.2 us
  transfers between devices with their start and end apart: 2, of which 2 were waited for; matrix products, arithmetic and copies ran while one was open for 1% of the time, Pallas kernels for 0%

commit v1 on v0

--- a/solution.py
+++ b/solution.py
@@ -78,7 +78,12 @@
         return focus_sector(pieces[0], start_angle[sector], ping_count[sector], stacked)[None]
 
     own_image = (lambda pieces: prepare(pieces, position))(
-        lax.all_to_all(raw_pings, "sector", split_axis=0, concat_axis=1, tiled=True)
+        jnp.concatenate(
+            lax.all_to_all(
+                jnp.stack(jnp.split(raw_pings, lax.axis_size("sector"), axis=0)), "sector", 0, 0
+            ),
+            axis=1,
+        )
     )
     other_image = shifted(own_image, "sector", -1)
     coherence, interferogram = compare(own_image[0], other_image[0], WIN)

time: 726 us -> 753 us (1.037)
  local copies, waits for them, and re-layouts: 168 us -> 193 us
    unnamed x5 -> x24, local copies, waits for them, and re-layouts: 83.1 us -> 108 us
  transfers between devices with their start and end apart: 2 -> 2, of which waited for: 2 -> 2; matrix products, arithmetic and copies ran while one was open for 1% -> 0% of each run, Pallas kernels for 0% -> 0%
where the time goes in v1:
time: 753 us; the launch traced here: 749 us
  other arithmetic  391 us (52%)
  local copies, waits for them, and re-layouts  193 us (26%)
  waiting for transfers between devices  130 us (17%)
  matrix products  17.5 us (2%)
  starting transfers between devices  17.2 us (2%)
    add x2, other arithmetic, window_sum(): total + lax.slice_in_dim(padded, offset, offset + length_axis, axis=axis)  279 us
    unnamed x24, local copies, waits for them, and re-layouts  108 us
    ppermute x1, waiting for transfers between devices, shifted(): return lax.ppermute(block, axis, route)  91.3 us
    reshape x1, local copies, waits for them, and re-layouts, focus_sector(): product = product.reshape(2, columns_count, 2, ranges_here)  42.6 us
    slice x1, local copies, waits for them, and re-layouts, focus_sector(): real_part = product[0, :, 0] - product[1, :, 1]  39.8 us
    all_to_all x1, waiting for transfers between devices, body(): lax.all_to_all(jnp.stack(jnp.split(raw_pings, lax.axis_size('sector'), ax...  38.3 us
    another operation x1, other arithmetic, compare(): jnp.stack([f_real * g_real + f_imag * g_imag, f_imag * g_real - f_real *...  23.4 us
    reduce_sum x1, other arithmetic, focus_sector(): mean_power = jnp.mean(real_part * real_part + imag_part * imag_part, axis=0)  19.2 us
  transfers between devices with their start and end apart: 2, of which 2 were waited for; matrix products, arithmetic and copies ran while one was open for 0% of the time, Pallas kernels for 0%

profile of v1, /device:TPU:0, one launch (start us, length us, event | category | flops | bytes accessed | tf_op | source)
XLA Modules:
  0.0 749.1 jit_solution(8647365512729383399)
XLA Ops:
  0.6 0.0 copy-start
  0.6 0.0 copy-start.1
  0.6 1.7 bitcast_dynamic-update-slice_fusion.15
  2.3 1.6 bitcast_dynamic-update-slice_fusion.14
  4.0 1.6 bitcast_dynamic-update-slice_fusion.13
  5.6 1.6 bitcast_dynamic-update-slice_fusion.12
  7.3 1.6 bitcast_dynamic-update-slice_fusion.11
  8.9 1.6 bitcast_dynamic-update-slice_fusion.10
  10.6 1.6 bitcast_dynamic-update-slice_fusion.9
  12.2 1.6 bitcast_dynamic-update-slice_fusion.8
  13.9 1.6 bitcast_dynamic-update-slice_fusion.7
  15.5 1.6 bitcast_dynamic-update-slice_fusion.6
  17.2 1.6 bitcast_dynamic-update-slice_fusion.5
  18.8 1.6 bitcast_dynamic-update-slice_fusion.4
  20.5 1.6 bitcast_dynamic-update-slice_fusion.3
  22.1 1.6 bitcast_dynamic-update-slice_fusion.2
  23.8 1.6 bitcast_dynamic-update-slice_fusion.1
  25.4 1.6 bitcast_dynamic-update-slice_fusion
  27.1 7.4 all-to-all-start
  34.5 0.0 copy-done
  34.5 0.6 dynamic_slice.6
  35.1 0.0 copy-done.1
  35.1 0.7 dynamic_slice.7
  35.7 0.7 fusion.37
  36.4 0.7 fusion.38
  37.1 38.3 %all-to-all-done = bf16[16,1,32,2,1024]{4,3,2,1,0:T(2,128)(2,1)S(1)} async-done(((bf16[16,1,32,2,1024]{4,3,2,1,0:T(2,128)(2,1)}), bf16[16,1,32,2,1024]{4,3,2,1,0:T(2,128)(2,1)S(1)}, u32[]{:S(2)}, u32[]{:S(2)}) %all-to-all-start) | async-done | bytes 2097184 | tf_op jit(solution)/shard_map/all_to_all | solution.py:82
  75.5 1.9 broadcast_multiply_fusion
  77.4 0.6 copy.14
  78.0 17.5 %convolution_bitcast_fusion = f32[4096,2048]{0,1:T(8,128)} fusion(bf16[512,2048]{1,0:T(8,128)(2,1)S(1)} %bitcast.84, bf16[4096,512]{1,0:T(8,128)(2,1)} %bitcast.85), kind=kOutput, calls=%fused_computation.23 | convolution fusion | flops 8589934592 | bytes 39845888 | tf_op jit(solution)/shard_map/dot_general | solution.py:21
  95.5 42.6 %reshape.406 = f32[2,2048,2,1024]{1,0,3,2:T(2,128)} reshape(f32[4096,2048]{0,1:T(8,128)} %convolution_bitcast_fusion) | data formatting | bytes 67108864 | tf_op jit(solution)/shard_map/reshape | solution.py:24
  138.1 39.8 %fusion.42 = (f32[1,2048,1,1024]{1,0,3,2:T(1,128)}, f32[1,2048,1,1024]{1,0,3,2:T(1,128)}, f32[1,2048,1,1024]{1,0,3,2:T(1,128)}, f32[1,2048,1,1024]{1,0,3,2:T(1,128)}) fusion(f32[2,2048,2,1024]{1,0,3,2:T(2,128)} %reshape.406), kind=kLoop, calls=%fused_computation.96 | loop fusion | bytes 67108864 | tf_op jit(solution)/shard_map/slice | solution.py:25
  177.9 20.7 %copy.10 = f32[1,2048,1,1024]{3,1,2,0:T(8,128)} copy(f32[1,2048,1,1024]{1,0,3,2:T(1,128)} %get-tuple-element.10) | data formatting | bytes 16777216
  198.6 20.7 %copy.11 = f32[1,2048,1,1024]{3,1,2,0:T(8,128)} copy(f32[1,2048,1,1024]{1,0,3,2:T(1,128)} %get-tuple-element.8) | data formatting | bytes 16777216
  219.3 20.5 %copy.12 = f32[1,2048,1,1024]{3,1,2,0:T(8,128)} copy(f32[1,2048,1,1024]{1,0,3,2:T(1,128)} %get-tuple-element.9) | data formatting | bytes 16777216
  239.8 20.5 %copy.13 = f32[1,2048,1,1024]{3,1,2,0:T(8,128)} copy(f32[1,2048,1,1024]{1,0,3,2:T(1,128)} %get-tuple-element.11) | data formatting | bytes 16777216
  260.4 19.2 %add_reduce_fusion = (f32[1024]{0:T(1024)S(1)}, f32[1,2048,1,1024]{3,1,2,0:T(8,128)}, f32[1,2048,1,1024]{3,1,2,0:T(8,128)}) fusion(f32[1,2048,1,1024]{3,1,2,0:T(8,128)} %copy.12, f32[1,2048,1,1024]{3,1,2,0:T(8,128)} %copy.13, f32[1,2048,1,1024]{3,1,2,0:T(8,128)} %copy.10, f32[1,2048,1,1024]{3,1,2,0:T(8,128)} %copy.11), kind=kLoop, calls=%fused_computation.64 | loop fusion | flops 12581888 | bytes 50335744 | tf_op jit(solution)/shard_map/reduce_sum | solution.py:32
  279.6 8.6 %multiply_convert_fusion.1 = (bf16[1,2048,1,1024]{3,1,2,0:T(8,128)(2,1)S(1)}, bf16[1,2048,1,1024]{3,1,2,0:T(8,128)(2,1)}) fusion(f32[1,2048,1,1024]{3,1,2,0:T(8,128)} %get-tuple-element.6, f32[1,2048,1,1024]{3,1,2,0:T(8,128)} %get-tuple-element.7, f32[1024]{0:T(1024)S(1)} %add_rsqrt_fusion, f32[2048]{0:T(1024)S(1)} %get-tuple-element.17, ...), kind=kLoop, calls=%fused_computation.63 | loop fusion | flops 20971520 | bytes 25186304 | tf_op jit(solution)/shard_map/convert
  288.2 6.2 pad_maximum_fusion.1
  294.4 9.8 %collective-permute-start = (bf16[1,2048,2,1024]{3,1,2,0:T(8,128)(2,1)}, bf16[1,2048,2,1024]{3,1,2,0:T(8,128)(2,1)S(1)}, u32[]{:S(2)}, u32[]{:S(2)}) collective-permute-start(bf16[1,2048,2,1024]{3,1,2,0:T(8,128)(2,1)} %pad_maximum_fusion.1), channel_id=1, source_target_pairs={{1,0},{2,1},{3,2},{4,3},{5,4},{6,5},{7,6},{8,7},{9,8},{10,9},{11,1... | collective-permute-start | bytes 25165832 | tf_op jit(solution)/shard_map/ppermute | solution.py:12
  304.3 91.3 %collective-permute-done = bf16[1,2048,2,1024]{3,1,2,0:T(8,128)(2,1)S(1)} collective-permute-done((bf16[1,2048,2,1024]{3,1,2,0:T(8,128)(2,1)}, bf16[1,2048,2,1024]{3,1,2,0:T(8,128)(2,1)S(1)}, u32[]{:S(2)}, u32[]{:S(2)}) %collective-permute-start) | collective-permute-done | bytes 8388640 | tf_op jit(solution)/shard_map/ppermute | solution.py:12
  395.5 13.3 %fusion.14 = (f32[1,2048,1024]{2,1,0:T(8,128)}, bf16[2048,1,1024]{2,0,1:T(8,128)(2,1)S(1)}, bf16[2048,1,1024]{2,0,1:T(8,128)(2,1)}) fusion(bf16[2048,2,1024]{2,0,1:T(8,128)(2,1)S(1)} %bitcast.81, f32[1024]{0:T(1024)S(1)} %add_rsqrt_fusion, f32[2048]{0:T(1024)S(1)} %get-tuple-element.17, f32[1,2048,1,1024]{3,1,2,0:T(8,128)} %get-tuple-element.7, ...), kind=kLoop, calls=%fused_computation.37 | loop fusion | flops 35651584 | bytes 41963520 | tf_op jit(solution)/shard_map/add | solution.py:58
  408.8 11.1 %fusion.18 = (f32[1,2048,1024]{2,1,0:T(8,128)}, f32[1,2048,1024]{2,1,0:T(8,128)}, f32[1,2048,1024]{2,1,0:T(8,128)}) fusion(bf16[2048,1,1024]{2,0,1:T(8,128)(2,1)S(1)} %get-tuple-element.3, bf16[2048,1,1024]{2,0,1:T(8,128)(2,1)} %get-tuple-element.4, bf16[2048,2,1024]{2,0,1:T(8,128)(2,1)S(1)} %bitcast.82), kind=kLoop, calls=%fused_computation.41 | loop fusion | flops 27262976 | bytes 41943040 | tf_op jit(solution)/shard_map/sub | solution.py:59
  420.0 23.4 %pad_maximum_fusion = f32[4,2048,1024]{2,1,0:T(8,128)} fusion(f32[1,2048,1024]{2,1,0:T(8,128)} %get-tuple-element.15, f32[1,2048,1024]{2,1,0:T(8,128)} %get-tuple-element.16, f32[1,2048,1024]{2,1,0:T(8,128)} %get-tuple-element.14, f32[1,2048,1024]{2,1,0:T(8,128)} %get-tuple-element.2), kind=kLoop, calls=%fused_computation.16 | loop fusion | flops 25165824 | bytes 67108864 | tf_op jit(solution)/shard_map/stack | solution.py:56
  443.4 131.7 %slice_add_fusion = f32[4,2048,1024]{2,1,0:T(8,128)} fusion(f32[4,2048,1024]{2,1,0:T(8,128)} %pad_maximum_fusion), kind=kLoop, calls=%fused_computation.17 | loop fusion | flops 67108864 | bytes 67108864 | tf_op jit(solution)/shard_map/add | solution.py:47
  575.1 147.6 %fusion.7 = f32[4,2048,1024]{2,1,0:T(8,128)} fusion(f32[4,2048,1024]{2,1,0:T(8,128)} %slice_add_fusion), kind=kLoop, calls=%fused_computation.15 | loop fusion | flops 67108864 | bytes 67108864 | tf_op jit(solution)/shard_map/add | solution.py:47
  722.7 9.6 %fusion.19 = bf16[1,2,2048,1024]{3,2,1,0:T(8,128)(2,1)} fusion(f32[4,2048,1024]{2,1,0:T(8,128)} %fusion.7), kind=kLoop, calls=%fused_computation.42 | loop fusion | flops 8388608 | bytes 25165824 | tf_op jit(solution)/shard_map/broadcast_in_dim | solution.py:90
  732.3 16.7 %fusion.22 = f32[1,2048,1024]{2,1,0:T(8,128)} fusion(f32[4,2048,1024]{2,1,0:T(8,128)} %fusion.7), kind=kLoop, calls=%fused_computation.46 | loop fusion | flops 12582912 | bytes 41943040 | tf_op jit(solution)/shard_map/div | solution.py:68
  (1 shorter events, 0.0 us)
Async XLA Ops:
  0.6 33.9 %copy-start = (s32[16]{0:T(128)S(1)}, s32[16]{0:T(128)}, u32[]{:S(2)}) copy-start(s32[16]{0:T(128)} %param.7) | copy-start | bytes 196
  0.6 34.4 %copy-start.1 = (s32[16]{0:T(128)S(1)}, s32[16]{0:T(128)}, u32[]{:S(2)}) copy-start(s32[16]{0:T(128)} %param.6) | copy-start | bytes 196
  27.1 48.4 %all-to-all-start = ((bf16[16,1,32,2,1024]{4,3,2,1,0:T(2,128)(2,1)}), bf16[16,1,32,2,1024]{4,3,2,1,0:T(2,128)(2,1)S(1)}, u32[]{:S(2)}, u32[]{:S(2)}) async-start(bf16[16,1,32,2,1024]{4,3,2,1,0:T(2,128)(2,1)} %bitcast_dynamic-update-slice_fusion), calls=%async_computation | async-start | bytes 4194304 | tf_op jit(solution)/shard_map/all_to_all | solution.py:82
  294.4 101.1 %collective-permute-start = (bf16[1,2048,2,1024]{3,1,2,0:T(8,128)(2,1)}, bf16[1,2048,2,1024]{3,1,2,0:T(8,128)(2,1)S(1)}, u32[]{:S(2)}, u32[]{:S(2)}) collective-permute-start(bf16[1,2048,2,1024]{3,1,2,0:T(8,128)(2,1)} %pad_maximum_fusion.1), channel_id=1, source_target_pairs={{1,0},{2,1},{3,2},{4,3},{5,4},{6,5},{7,6},{8,7},{9,8},{10,9},{11,1... | collective-permute-start | bytes 25165832 | tf_op jit(solution)/shard_map/ppermute | solution.py:12
